TPU v7x, 256 devices: a whole 4x4x8 slice. The times are simulated.
256 devices in a mesh: row: 16 (over z, core), col: 16 (over x, y).
Axes of the slice: x: 4, y: 4, z: 8, core: 2. Of those that a mesh axis runs over, the one named last changes fastest.
Arguments:
- inputs: bfloat16 [4096, 18432], P('col', 'row'), may hold values from -6 to 6
- out_grads: bfloat16 [4096, 18432], P('row', 'col'), may hold values from -0.09375 to 0.09375
- range_test: float32 [18432, 128], P('col'), may hold values from -0.046875 to 0.046875
- corange_test: float32 [256, 18432], P(None, 'row'), may hold values from -0.046875 to 0.046875
Outputs:
- range_sketch: float32 [18432, 128], P('row')
- corange_sketch: float32 [256, 18432], P(None, 'col')
- residual: float32 [18432, 18432], P('row', 'col')
All inputs are finite; a program needn't handle non-finite values.
Results may differ from a plain program's by a relative error of at most 0.0003.
Values may be sent and summed in bfloat16 or wider, within the bound.
A program may use at most 128 MiB of HBM per device.

v0:
```python
import jax
import jax.numpy as jnp
from jax import lax
from jax.sharding import PartitionSpec as P

highest = lax.Precision.HIGHEST


def token_product(left_rows, right_rows):
    return lax.dot_general(
        left_rows, right_rows, (((0,), (0,)), ((), ())), preferred_element_type=jnp.float32
    )


def exact_product(left_side, right_side):
    return jnp.dot(left_side, right_side, precision=highest, preferred_element_type=jnp.float32)


def per_device(inputs, out_grads, range_test, corange_test):
    grads_all = lax.all_gather(out_grads, "row", axis=0, tiled=True)
    gradient = token_product(lax.all_gather(inputs, "col", axis=0, tiled=True), grads_all)
    range_sketch = lax.psum(exact_product(gradient, range_test), "col")
    corange_sketch = lax.psum(exact_product(corange_test, gradient), "row")
    core_input = lax.psum(exact_product(corange_test, range_sketch), "row")
    gram_matrix = lax.dot_general(
        core_input,
        core_input,
        (((0,), (0,)), ((), ())),
        precision=highest,
        preferred_element_type=jnp.float32,
    )
    factor_low = jnp.linalg.cholesky(gram_matrix)
    core_map = jax.scipy.linalg.cho_solve((factor_low, True), core_input.T)
    project = exact_product(core_map, corange_sketch)
    residual = gradient - exact_product(range_sketch, project)
    return (range_sketch, corange_sketch, residual)


def solution(mesh):
    placed = (P("col", "row"), P("row", "col"), P("col", None), P(None, "row"))
    return jax.shard_map(
        per_device,
        mesh=mesh,
        in_specs=placed,
        out_specs=(P("row", None), P(None, "col"), P("row", "col")),
        check_vma=False,
    )
```

profile of v0, /device:TPU:1, one launch (start us, length us, event | category | flops | bytes accessed | tf_op | source)
XLA Modules:
  0.0 438.1 jit_solution(6629856623916740087)
XLA Ops:
  7.2 0.0 copy-start
  7.2 0.0 all-gather.3.cloned.1.call-start
  7.2 0.7 all-gather.3.cloned.1.call-update
  7.9 0.0 all-gather.5.cloned.1.call-start
  8.0 0.7 all-gather.5.cloned.1.call-update
  8.7 0.0 copy-start.3
  8.7 0.0 all-reduce.4.cloned.1.call-start
  8.7 86.0 %all-gather.3.cloned.1.call-done = bf16[4096,1152]{1,0:T(8,128)(2,1)} async-done(((bf16[256,1152]{1,0:T(8,128)(2,1)}), bf16[4096,1152]{1,0:T(8,128)(2,1)}) %all-gather.3.cloned.1.call-update) | async-done | bytes 9437200 | tf_op jit(solution)/shard_map/all_gather | solution.py:21
  94.7 63.0 %all-gather.5.cloned.1.call-done = bf16[4096,1152]{1,0:T(8,128)(2,1)} async-done(((bf16[256,1152]{1,0:T(8,128)(2,1)}), bf16[4096,1152]{1,0:T(8,128)(2,1)}) %all-gather.5.cloned.1.call-update) | async-done | bytes 9437200 | tf_op jit(solution)/shard_map/all_gather | solution.py:20
  157.6 17.0 %fusion.6 = f32[1152,1152]{1,0:T(8,128)S(1)} fusion(bf16[4096,1152]{1,0:T(8,128)(2,1)} %all-gather.3.cloned.1.call-done, bf16[4096,1152]{1,0:T(8,128)(2,1)} %all-gather.5.cloned.1.call-done), kind=kOutput, calls=%fused_computation.15 | convolution fusion | flops 10871635968 | bytes 24182784 | tf_op jit(solution)/shard_map/dot_general | solution.py:10
  174.7 0.0 copy-start.1
  174.7 2.4 copy-done.1
  177.1 5.3 %fusion.7 = f32[1152,128]{1,0:T(8,128)} fusion(f32[1152,1152]{1,0:T(8,128)S(1)} %fusion.6, f32[1152,128]{1,0:T(8,128)S(1)} %copy-done.3), kind=kOutput, calls=%fused_computation.16 | convolution fusion | flops 2038431744 | bytes 6488064 | tf_op jit(solution)/shard_map/dot_general | solution.py:16
  182.4 0.0 all-reduce.4.cloned.1.call-update
  182.4 0.2 all-reduce.6.cloned.1.call-start
  182.7 12.0 %convolution_bitcast_fusion = f32[256,1152]{0,1:T(8,128)} fusion(f32[1152,1152]{1,0:T(8,128)} %copy-done.1, f32[256,1152]{1,0:T(8,128)S(1)} %copy-done), kind=kOutput, calls=%fused_computation.1 | convolution fusion | flops 4076863488 | bytes 7667712 | tf_op jit(solution)/shard_map/dot_general | solution.py:16
  194.6 79.5 %all-reduce.4.cloned.1.call-done = f32[1152,128]{1,0:T(8,128)} async-done(((f32[1152,128]{1,0:T(8,128)}), f32[1152,128]{1,0:T(8,128)}) %all-reduce.4.cloned.1.call-update) | async-done | bytes 589840 | tf_op jit(solution)/shard_map/psum | solution.py:22
  274.1 3.0 convolution_bitcast_fusion.1
  277.1 0.0 all-reduce.6.cloned.1.call-update
  277.1 114.8 %all-reduce.6.cloned.1.call-done = (f32[256,1152]{0,1:T(8,128)}, f32[256,128]{0,1:T(8,128)}) async-done(((f32[256,1152]{0,1:T(8,128)}, f32[256,128]{0,1:T(8,128)}), (f32[256,1152]{0,1:T(8,128)}, f32[256,128]{0,1:T(8,128)})) %all-reduce.6.cloned.1.call-update) | async-done | bytes 1310736 | tf_op jit(solution)/shard_map/psum | solution.py:23
  392.0 1.3 fusion.8
  393.2 0.1 copy.7
  393.3 11.9 %cholesky.16 = f32[128,128]{1,0:T(8,128)S(1)} custom-call(f32[128,128]{1,0:T(8,128)S(1)} %fusion.5), custom_call_target="Cholesky" | custom-call | tf_op jit(solution)/shard_map/jit(cholesky)/cholesky | solution.py:32
  405.3 0.6 compare_reduce_fusion
  405.9 0.7 fusion
  406.6 9.8 %custom-call.10 = f32[1,128,128]{1,2,0:T(8,128)S(1)} custom-call(f32[1,128,128]{2,1,0:T(8,128)S(1)} %fusion), custom_call_target="InvertDiagBlocksLowerTriangular" | custom-call | tf_op jit(solution)/shard_map/jit(_cho_solve)/triangular_solve | solution.py:33
  416.4 1.2 fusion.3
  417.6 0.3 fusion.1
  417.9 2.7 copy.8
  420.6 2.5 fusion.9
  423.1 7.7 %convolution_subtract_fusion = f32[1152,1152]{1,0:T(8,128)} fusion(f32[1152,1152]{1,0:T(8,128)} %copy-done.1, f32[1152,128]{1,0:T(8,128)S(1)} %copy-done.2, f32[128,1152]{1,0:T(8,128)S(1)} %fusion.9), kind=kOutput, calls=%fused_computation | convolution fusion | flops 2039758848 | bytes 11796480 | tf_op jit(solution)/shard_map/dot_general | solution.py:16
  430.8 0.8 copy.12
  (6 shorter events, 0.1 us)
Async XLA Ops:
  7.2 175.5 %copy-start = (f32[256,1152]{1,0:T(8,128)S(1)}, f32[256,1152]{1,0:T(8,128)}, u32[]{:S(2)}) copy-start(f32[256,1152]{1,0:T(8,128)} %param.7) | copy-start | bytes 3538948
  7.2 87.5 %all-gather.3.cloned.1.call-start = ((), (), s32[]{:S(2)}) async-start(), calls=%async_computation | async-start | bytes 10027008 | tf_op jit(solution)/shard_map/all_gather | solution.py:21
  7.9 149.7 %all-gather.5.cloned.1.call-start = ((), (), s32[]{:S(2)}) async-start(), calls=%async_computation.1 | async-start | bytes 10027008 | tf_op jit(solution)/shard_map/all_gather | solution.py:20
  8.7 168.4 %copy-start.3 = (f32[1152,128]{1,0:T(8,128)S(1)}, f32[1152,128]{1,0:T(8,128)}, u32[]{:S(2)}) copy-start(f32[1152,128]{1,0:T(8,128)} %param.6) | copy-start | bytes 1769476
  8.7 265.4 %all-reduce.4.cloned.1.call-start = ((), (), s32[]{:S(2)}) async-start(), calls=%async_computation.2 | async-start | bytes 1179648 | tf_op jit(solution)/shard_map/psum | solution.py:22
  174.7 2.4 copy-start.1
  182.4 209.6 %all-reduce.6.cloned.1.call-start = ((), (), s32[]{:S(2)}) async-start(), calls=%async_computation.3 | async-start | bytes 2621440 | tf_op jit(solution)/shard_map/psum | solution.py:23
  274.1 149.0 %copy-start.2 = (f32[1152,128]{1,0:T(8,128)S(1)}, f32[1152,128]{1,0:T(8,128)}, u32[]{:S(2)}) copy-start(f32[1152,128]{1,0:T(8,128)} %all-reduce.4.cloned.1.call-done) | copy-start | bytes 1769476
Sparse Core Ops, SparseCore 0:
  10.5 84.1 all-gather.2
  96.5 61.0 all-gather.4
  182.5 91.4 all-reduce.3
  277.3 114.6 all-reduce.5
where the time goes:
time: 438 us
  waiting for transfers between devices  345 us (79%)
  matrix products  50.3 us (11%)
  other arithmetic  23.1 us (5%)
  between operations  13.9 us (3%)
  local copies, waits for them, and re-layouts  5.95 us (1%)
    psum x1, waiting for transfers between devices, per_device(): corange_sketch = lax.psum(exact_product(corange_test, gradient), 'row')  115 us
    all_gather x1, waiting for transfers between devices, per_device(): lax.all_gather(inputs, 'col', axis=0, tiled=True)  86 us
    psum x1, waiting for transfers between devices, per_device(): range_sketch = lax.psum(exact_product(gradient, range_test), 'col')  79.5 us
    all_gather x1, waiting for transfers between devices, per_device(): grads_all = lax.all_gather(out_grads, 'row', axis=0, tiled=True)  63 us
    dot_general x5, matrix products, exact_product(): jnp.dot(left_side, right_side, precision=highest, preferred_element_type=...  30.5 us
    dot_general x1, matrix products, token_product(): lax.dot_general(left_rows, right_rows, (((0,), (0,)), ((), ())), preferre...  17 us
    another operation x3, other arithmetic, per_device(): factor_low = jnp.linalg.cholesky(gram_matrix)  12.6 us
    another operation x2, other arithmetic, per_device(): core_map = jax.scipy.linalg.cho_solve((factor_low, True), core_input.T)  10.5 us
  transfers between devices with their start and end apart: 4, of which 4 were waited for; matrix products, arithmetic and copies ran while one was open for 3% of the time, Pallas kernels for 0%

commit v1 on v0

--- a/solution.py
+++ b/solution.py
@@ -17,7 +17,12 @@
 
 
 def per_device(inputs, out_grads, range_test, corange_test):
-    grads_all = lax.all_gather(out_grads, "row", axis=0, tiled=True)
+    grads_all = jnp.concatenate(
+        lax.all_to_all(
+            jnp.stack([out_grads] * lax.axis_size("row"), 0), "row", split_axis=0, concat_axis=0
+        ),
+        0,
+    )
     gradient = token_product(lax.all_gather(inputs, "col", axis=0, tiled=True), grads_all)
     range_sketch = lax.psum(exact_product(gradient, range_test), "col")
     corange_sketch = lax.psum(exact_product(corange_test, gradient), "row")

time: 438 us -> 511 us (1.17)
  waiting for transfers between devices: 345 us -> 401 us
  starting transfers between devices: 0.34 us -> 10.3 us
  local copies, waits for them, and re-layouts: 5.95 us -> 12.1 us
    all_to_all x0 -> x1, waiting for transfers between devices: none -> 205 us  [per_device(): lax.all_to_all(jnp.stack([out_grads] * lax.axis_size('row'), 0), 'row', s...]
    all_gather x1, waiting for transfers between devices: 86 us -> 0.01 us  [per_device(): lax.all_gather(inputs, 'col', axis=0, tiled=True)]
    all_gather x1 -> x0, waiting for transfers between devices: 63 us -> none  [per_device(): grads_all = lax.all_gather(out_grads, 'row', axis=0, tiled=True)]
    all_to_all x0 -> x1, starting transfers between devices: none -> 9.97 us  [per_device(): lax.all_to_all(jnp.stack([out_grads] * lax.axis_size('row'), 0), 'row', s...]
    another operation x0 -> x1, local copies, waits for them, and re-layouts: none -> 6.15 us  [per_device(): jnp.stack([out_grads] * lax.axis_size('row'), 0)]
  transfers between devices with their start and end apart: 4 -> 4, of which waited for: 4 -> 3; matrix products, arithmetic and copies ran while one was open for 3% -> 2% of each run, Pallas kernels for 0% -> 0%
where the time goes in v1:
time: 511 us
  waiting for transfers between devices  401 us (78%)
  matrix products  50.3 us (10%)
  other arithmetic  23.1 us (5%)
  between operations  13.9 us (3%)
  local copies, waits for them, and re-layouts  12.1 us (2%)
  starting transfers between devices  10.3 us (2%)
    all_to_all x1, waiting for transfers between devices, per_device(): lax.all_to_all(jnp.stack([out_grads] * lax.axis_size('row'), 0), 'row', s...  205 us
    psum x1, waiting for transfers between devices, per_device(): corange_sketch = lax.psum(exact_product(corange_test, gradient), 'row')  115 us
    psum x1, waiting for transfers between devices, per_device(): range_sketch = lax.psum(exact_product(gradient, range_test), 'col')  80.8 us
    dot_general x5, matrix products, exact_product(): jnp.dot(left_side, right_side, precision=highest, preferred_element_type=...  30.5 us
    dot_general x1, matrix products, token_product(): lax.dot_general(left_rows, right_rows, (((0,), (0,)), ((), ())), preferre...  17.1 us
    another operation x3, other arithmetic, per_device(): factor_low = jnp.linalg.cholesky(gram_matrix)  12.6 us
    another operation x2, other arithmetic, per_device(): core_map = jax.scipy.linalg.cho_solve((factor_low, True), core_input.T)  10.5 us
  transfers between devices with their start and end apart: 4, of which 3 were waited for; matrix products, arithmetic and copies ran while one was open for 2% of the time, Pallas kernels for 0%

profile of v1, /device:TPU:1, one launch (start us, length us, event | category | flops | bytes accessed | tf_op | source)
XLA Modules:
  0.0 511.0 jit_solution(9506117028227731135)
XLA Ops:
  7.2 0.0 copy-start
  7.2 6.1 %stack.2 = bf16[16,256,1152]{2,1,0:T(8,128)(2,1)} broadcast(bf16[256,1152]{1,0:T(8,128)(2,1)} %param.5), dimensions={1,2} | broadcast | bytes 10027008 | tf_op jit(solution)/shard_map/stack | solution.py:22
  13.3 10.0 %all-to-all-start = ((bf16[16,256,1152]{2,1,0:T(8,128)(2,1)}), bf16[16,256,1152]{2,1,0:T(8,128)(2,1)}, u32[]{:S(2)}, u32[]{:S(2)}) async-start(bf16[16,256,1152]{2,1,0:T(8,128)(2,1)} %stack.2), calls=%async_computation | async-start | bytes 18874368 | tf_op jit(solution)/shard_map/all_to_all | solution.py:21
  23.3 0.0 all-gather.2.cloned.1.call-start
  23.3 0.7 all-gather.2.cloned.1.call-update
  24.0 0.0 all-reduce.4.cloned.1.call-start
  24.1 205.0 %all-to-all-done = bf16[16,256,1152]{2,1,0:T(8,128)(2,1)} async-done(((bf16[16,256,1152]{2,1,0:T(8,128)(2,1)}), bf16[16,256,1152]{2,1,0:T(8,128)(2,1)}, u32[]{:S(2)}, u32[]{:S(2)}) %all-to-all-start) | async-done | bytes 9437216 | tf_op jit(solution)/shard_map/all_to_all | solution.py:21
  229.1 17.1 %fusion.6 = f32[1152,1152]{1,0:T(8,128)S(1)} fusion(bf16[4096,1152]{1,0:T(8,128)(2,1)} %all-gather.2.cloned.1.call-done, bf16[4096,1152]{1,0:T(8,128)(2,1)} %bitcast), kind=kOutput, calls=%fused_computation.15 | convolution fusion | flops 10871635968 | bytes 24182784 | tf_op jit(solution)/shard_map/dot_general | solution.py:10
  246.2 0.0 copy-start.1
  246.2 2.4 copy-done.1
  248.6 0.0 copy-done.3
  248.6 5.3 %fusion.7 = f32[1152,128]{1,0:T(8,128)} fusion(f32[1152,1152]{1,0:T(8,128)S(1)} %fusion.6, f32[1152,128]{1,0:T(8,128)S(1)} %copy-done.3), kind=kOutput, calls=%fused_computation.16 | convolution fusion | flops 2038431744 | bytes 6488064 | tf_op jit(solution)/shard_map/dot_general | solution.py:16
  253.9 0.0 all-reduce.4.cloned.1.call-update
  253.9 0.2 all-reduce.6.cloned.1.call-start
  254.2 0.0 copy-done
  254.2 12.0 %convolution_bitcast_fusion = f32[256,1152]{0,1:T(8,128)} fusion(f32[1152,1152]{1,0:T(8,128)} %copy-done.1, f32[256,1152]{1,0:T(8,128)S(1)} %copy-done), kind=kOutput, calls=%fused_computation.1 | convolution fusion | flops 4076863488 | bytes 7667712 | tf_op jit(solution)/shard_map/dot_general | solution.py:16
  266.1 80.8 %all-reduce.4.cloned.1.call-done = f32[1152,128]{1,0:T(8,128)} async-done(((f32[1152,128]{1,0:T(8,128)}), f32[1152,128]{1,0:T(8,128)}) %all-reduce.4.cloned.1.call-update) | async-done | bytes 589840 | tf_op jit(solution)/shard_map/psum | solution.py:27
  347.0 3.0 convolution_bitcast_fusion.1
  350.0 0.0 all-reduce.6.cloned.1.call-update
  350.0 114.8 %all-reduce.6.cloned.1.call-done = (f32[256,1152]{0,1:T(8,128)}, f32[256,128]{0,1:T(8,128)}) async-done(((f32[256,1152]{0,1:T(8,128)}, f32[256,128]{0,1:T(8,128)}), (f32[256,1152]{0,1:T(8,128)}, f32[256,128]{0,1:T(8,128)})) %all-reduce.6.cloned.1.call-update) | async-done | bytes 1310736 | tf_op jit(solution)/shard_map/psum | solution.py:28
  464.9 1.3 fusion.8
  466.1 0.1 copy.7
  466.3 11.9 %cholesky.16 = f32[128,128]{1,0:T(8,128)S(1)} custom-call(f32[128,128]{1,0:T(8,128)S(1)} %fusion.5), custom_call_target="Cholesky" | custom-call | tf_op jit(solution)/shard_map/jit(cholesky)/cholesky | solution.py:37
  478.2 0.6 compare_reduce_fusion
  478.9 0.7 fusion
  479.5 9.8 %custom-call.10 = f32[1,128,128]{1,2,0:T(8,128)S(1)} custom-call(f32[1,128,128]{2,1,0:T(8,128)S(1)} %fusion), custom_call_target="InvertDiagBlocksLowerTriangular" | custom-call | tf_op jit(solution)/shard_map/jit(_cho_solve)/triangular_solve | solution.py:38
  489.3 1.2 fusion.3
  490.6 0.3 fusion.1
  490.8 2.7 copy.8
  493.5 2.5 fusion.9
  496.0 7.7 %convolution_subtract_fusion = f32[1152,1152]{1,0:T(8,128)} fusion(f32[1152,1152]{1,0:T(8,128)} %copy-done.1, f32[1152,128]{1,0:T(8,128)S(1)} %copy-done.2, f32[128,1152]{1,0:T(8,128)S(1)} %fusion.9), kind=kOutput, calls=%fused_computation | convolution fusion | flops 2039758848 | bytes 11796480 | tf_op jit(solution)/shard_map/dot_general | solution.py:16
  503.7 0.8 copy.12
  (6 shorter events, 0.1 us)
Async XLA Ops:
  7.2 247.0 %copy-start = (f32[256,1152]{1,0:T(8,128)S(1)}, f32[256,1152]{1,0:T(8,128)}, u32[]{:S(2)}) copy-start(f32[256,1152]{1,0:T(8,128)} %param.7) | copy-start | bytes 3538948
  13.3 215.8 %all-to-all-start = ((bf16[16,256,1152]{2,1,0:T(8,128)(2,1)}), bf16[16,256,1152]{2,1,0:T(8,128)(2,1)}, u32[]{:S(2)}, u32[]{:S(2)}) async-start(bf16[16,256,1152]{2,1,0:T(8,128)(2,1)} %stack.2), calls=%async_computation | async-start | bytes 18874368 | tf_op jit(solution)/shard_map/all_to_all | solution.py:21
  23.3 205.8 %all-gather.2.cloned.1.call-start = ((), (), s32[]{:S(2)}) async-start(), calls=%async_computation.1 | async-start | bytes 10027008 | tf_op jit(solution)/shard_map/all_gather | solution.py:26
  24.0 322.9 %all-reduce.4.cloned.1.call-start = ((), (), s32[]{:S(2)}) async-start(), calls=%async_computation.2 | async-start | bytes 1179648 | tf_op jit(solution)/shard_map/psum | solution.py:27
  229.1 19.5 %copy-start.3 = (f32[1152,128]{1,0:T(8,128)S(1)}, f32[1152,128]{1,0:T(8,128)}, u32[]{:S(2)}) copy-start(f32[1152,128]{1,0:T(8,128)} %param.6) | copy-start | bytes 1769476
  246.2 2.4 copy-start.1
  253.9 210.9 %all-reduce.6.cloned.1.call-start = ((), (), s32[]{:S(2)}) async-start(), calls=%async_computation.3 | async-start | bytes 2621440 | tf_op jit(solution)/shard_map/psum | solution.py:28
  347.0 149.0 %copy-start.2 = (f32[1152,128]{1,0:T(8,128)S(1)}, f32[1152,128]{1,0:T(8,128)}, u32[]{:S(2)}) copy-start(f32[1152,128]{1,0:T(8,128)} %all-reduce.4.cloned.1.call-done) | copy-start | bytes 1769476
Sparse Core Ops, SparseCore 0:
  26.6 81.4 all-gather.1
  254.1 92.8 all-reduce.3
  350.2 114.6 all-reduce.5
